TPU v7x, 32 devices: a whole 2x2x4 slice. The times are simulated.
32 devices in a mesh: section: 4 (over z), dp: 4 (over y, x), tensor: 2 (over core).
Axes of the slice: x: 2, y: 2, z: 4, core: 2. Of those that a mesh axis runs over, the one named last changes fastest.
Arguments:
- sent_out: bfloat16 [4, 2, 768, 4096], P('section', None, 'dp', 'tensor'), may hold values from -6 to 6
- sent_back: bfloat16 [4, 2, 768, 4096], P('section', None, 'dp', 'tensor'), may hold values from -6 to 6
- sent_grad: bfloat16 [4, 2, 768, 4096], P('section', None, 'dp', 'tensor'), may hold values from -6 to 6
- lengths: int32 [4, 4], P('section', 'dp'), may hold values from 48 to 192
- weight: bfloat16 [4, 4096, 4096], P('section', 'dp', 'tensor'), may hold values from -0.09375 to 0.09375
Outputs:
- emitted: bfloat16 [4, 2, 768, 4096], P('section', None, 'dp', 'tensor')
- rebuilt: bfloat16 [4, 2, 768, 4096], P('section', None, 'dp', 'tensor')
- input_grad: bfloat16 [4, 2, 768, 4096], P('section', None, 'dp', 'tensor')
- weight_grad: bfloat16 [4, 4096, 4096], P('section', 'dp', 'tensor')
All inputs are finite; a program needn't handle non-finite values.
Results may differ from a plain program's by a relative error of at most 0.0075.
Values may be sent and summed in bfloat16 or wider, within the bound.
A program may use at most 128 MiB of HBM per device.

v0:
```python
import jax
import jax.numpy as jnp
from jax import lax
from jax.sharding import PartitionSpec as P


def shifted(block, axis, distance):
    devices = range(lax.axis_size(axis))
    route = [((i - distance) % len(devices), i) for i in devices]
    return lax.ppermute(block, axis, route)


def across_rows(left, right):
    return lax.dot_general(
        left, right, (((0,), (0,)), ((), ())), preferred_element_type=jnp.float32
    )


def slope(hidden):
    sigma = jax.nn.sigmoid(hidden)
    return sigma * (1.0 + hidden * (1.0 - sigma))


def local(sent_out, sent_back, sent_grad, lengths, weight):
    token_rows = sent_out.shape[2]
    local_weight = weight[0]
    whole_weight = lax.all_gather(local_weight, "dp", axis=0, tiled=True)
    inbound = shifted(sent_out, "section", 1)
    upper_in = inbound[0, 0]
    lower_in = inbound[0, 1]
    upper_full = lax.all_gather(upper_in, "tensor", axis=1, tiled=True)
    pre = jnp.dot(upper_full, whole_weight, preferred_element_type=jnp.float32)
    upper_out = (lower_in.astype(jnp.float32) + jax.nn.silu(pre)).astype(jnp.bfloat16)
    emitted = jnp.stack([upper_out, upper_in])[None]
    back, incoming = shifted((sent_back, sent_grad), "section", -1)
    back_upper = back[0, 0]
    back_lower = back[0, 1]
    lower_full = lax.all_gather(back_lower, "tensor", axis=1, tiled=True)
    pre_held = jnp.dot(lower_full, whole_weight, preferred_element_type=jnp.float32)
    rebuilt_lower = (back_upper.astype(jnp.float32) - jax.nn.silu(pre_held)).astype(jnp.bfloat16)
    rebuilt = jnp.stack([back_lower, rebuilt_lower])[None]
    keep = (jnp.arange(token_rows, dtype=jnp.int32) < lengths[0, 0])[:, None]
    zero = jnp.zeros((), jnp.bfloat16)
    dupper = jnp.where(keep, incoming[0, 0], zero)
    dlower = jnp.where(keep, incoming[0, 1], zero)
    hidden = (dupper.astype(jnp.float32) * slope(pre_held)).astype(jnp.bfloat16)
    terms = lax.dot_general(
        hidden, whole_weight, (((1,), (1,)), ((), ())), preferred_element_type=jnp.float32
    )
    through = lax.psum_scatter(
        terms.astype(jnp.bfloat16), "tensor", scatter_dimension=1, tiled=True
    ).astype(jnp.float32)
    dupper_in = (dlower.astype(jnp.float32) + through).astype(jnp.bfloat16)
    grads_out = jnp.stack([dupper_in, dupper])[None]
    held_share = lax.all_to_all(lower_full, "dp", split_axis=1, concat_axis=0, tiled=True)
    hidden_all = lax.all_gather(hidden, "dp", axis=0, tiled=True)
    weight_grad = across_rows(held_share, hidden_all).astype(jnp.bfloat16)[None]
    rebuilt, grads_out, weight_grad = (rebuilt, grads_out, weight_grad)
    return (emitted, rebuilt, grads_out, weight_grad)


def solution(mesh):
    return jax.shard_map(
        local,
        mesh=mesh,
        in_specs=(
            P("section", None, "dp", "tensor"),
            P("section", None, "dp", "tensor"),
            P("section", None, "dp", "tensor"),
            P("section", "dp"),
            P("section", "dp", "tensor"),
        ),
        out_specs=(
            P("section", None, "dp", "tensor"),
            P("section", None, "dp", "tensor"),
            P("section", None, "dp", "tensor"),
            P("section", "dp", "tensor"),
        ),
        check_vma=False,
    )
```

profile of v0, /device:TPU:0, one launch (start us, length us, event | category | flops | bytes accessed | tf_op | source)
XLA Modules:
  0.0 327.9 jit_solution(17365934528555776995)
XLA Ops:
  7.2 5.1 %collective-permute-start.1 = (bf16[1,2,192,2048]{3,2,1,0:T(8,128)(2,1)}, bf16[1,2,192,2048]{3,2,1,0:T(8,128)(2,1)S(1)}, u32[]{:S(2)}, u32[]{:S(2)}) collective-permute-start(bf16[1,2,192,2048]{3,2,1,0:T(8,128)(2,1)} %param.6), channel_id=1, source_target_pairs={{8,0},{16,8},{24,16},{0,24},{9,1},{17,9},{25,17},{1,25},{10,2},{18... | collective-permute-start | bytes 4718600 | tf_op jit(solution)/shard_map/ppermute | solution.py:10
  12.3 34.0 %collective-permute-done.1 = bf16[1,2,192,2048]{3,2,1,0:T(8,128)(2,1)S(1)} collective-permute-done((bf16[1,2,192,2048]{3,2,1,0:T(8,128)(2,1)}, bf16[1,2,192,2048]{3,2,1,0:T(8,128)(2,1)S(1)}, u32[]{:S(2)}, u32[]{:S(2)}) %collective-permute-start.1) | collective-permute-done | bytes 1572896 | tf_op jit(solution)/shard_map/ppermute | solution.py:10
  46.3 1.1 copy-done.5
  47.5 1.1 slice_bitcast_fusion.3
  48.5 0.0 all-gather.12.cloned.1.call-start
  48.6 0.7 all-gather.12.cloned.1.call-update
  49.3 0.4 collective-permute-start
  49.7 3.9 %collective-permute-start.2 = (bf16[1,2,192,2048]{3,2,1,0:T(8,128)(2,1)}, bf16[1,2,192,2048]{3,2,1,0:T(8,128)(2,1)S(1)}, u32[]{:S(2)}, u32[]{:S(2)}) collective-permute-start(bf16[1,2,192,2048]{3,2,1,0:T(8,128)(2,1)} %param.7), channel_id=1, source_target_pairs={{8,0},{16,8},{24,16},{0,24},{9,1},{17,9},{25,17},{1,25},{10,2},{18... | collective-permute-start | bytes 4718600 | tf_op jit(solution)/shard_map/ppermute | solution.py:10
  54.3 34.9 %collective-permute-done = bf16[1,2,192,2048]{3,2,1,0:T(8,128)(2,1)} collective-permute-done((bf16[1,2,192,2048]{3,2,1,0:T(8,128)(2,1)}, bf16[1,2,192,2048]{3,2,1,0:T(8,128)(2,1)}, u32[]{:S(2)}, u32[]{:S(2)}) %collective-permute-start) | collective-permute-done | bytes 1572896 | tf_op jit(solution)/shard_map/ppermute | solution.py:10
  89.2 2.5 fusion.17
  91.7 0.0 reduce-scatter.2.cloned.1.call-start
  91.7 26.9 %collective-permute-done.2 = bf16[1,2,192,2048]{3,2,1,0:T(8,128)(2,1)S(1)} collective-permute-done((bf16[1,2,192,2048]{3,2,1,0:T(8,128)(2,1)}, bf16[1,2,192,2048]{3,2,1,0:T(8,128)(2,1)S(1)}, u32[]{:S(2)}, u32[]{:S(2)}) %collective-permute-start.2) | collective-permute-done | bytes 1572896 | tf_op jit(solution)/shard_map/ppermute | solution.py:10
  118.7 102.0 %all-gather.12.cloned.1.call-done = bf16[1,4096,2048]{2,1,0:T(8,128)(2,1)} async-done(((bf16[1,1024,2048]{2,1,0:T(8,128)(2,1)}), bf16[1,4096,2048]{2,1,0:T(8,128)(2,1)}) %all-gather.12.cloned.1.call-update) | async-done | bytes 16777232 | tf_op jit(solution)/shard_map/all_gather | solution.py:27
  220.7 11.4 %multiply_convert_fusion = (bf16[192,2048]{1,0:T(8,128)(2,1)S(1)}, bf16[1,192,2048]{2,1,0:T(8,128)(2,1)}) fusion(pred[192]{0:T(512)(128)(4,1)S(1)} %iota_compare_fusion, bf16[1,2,192,2048]{3,2,1,0:T(8,128)(2,1)S(1)} %collective-permute-done.2, bf16[1,2,192,2048]{3,2,1,0:T(8,128)(2,1)} %copy-done.5, ...), kind=kOutput, calls=%fused_computation.18 | convolution fusion | flops 3227123712 | bytes 21496000 | tf_op jit(solution)/shard_map/dot_general | solution.py:39
  232.0 12.8 %fusion.6 = bf16[192,4096]{1,0:T(8,128)(2,1)} fusion(bf16[192,2048]{1,0:T(8,128)(2,1)S(1)} %get-tuple-element.12, bf16[1,4096,2048]{2,1,0:T(8,128)(2,1)} %all-gather.12.cloned.1.call-done), kind=kOutput, calls=%fused_computation.6 | convolution fusion | flops 3222011904 | bytes 19136512 | tf_op jit(solution)/shard_map/dot_general | solution.py:47
  244.9 0.0 all-gather.8.cloned.1.call-start
  244.9 0.5 all-gather.8.cloned.1.call-update
  245.5 0.1 bitcast_select_fusion
  245.6 2.9 all_to_all.14
  248.5 1.7 copy.10
  250.2 4.5 %all-to-all-start = ((bf16[192,4,1024]{2,0,1:T(8,128)(2,1)}), bf16[192,4,1024]{2,0,1:T(8,128)(2,1)}, u32[]{:S(2)}, u32[]{:S(2)}) async-start(bf16[192,4,1024]{2,0,1:T(8,128)(2,1)} %copy.10), calls=%async_computation.1 | async-start | bytes 3145728 | tf_op jit(solution)/shard_map/all_to_all | solution.py:55
  254.8 10.0 %fusion.15 = bf16[1,192,2048]{2,1,0:T(8,128)(2,1)S(1)} fusion(bf16[1,2,192,2048]{3,2,1,0:T(8,128)(2,1)} %collective-permute-done, bf16[1,4096,2048]{2,1,0:T(8,128)(2,1)} %all-gather.12.cloned.1.call-done, bf16[1,1,192,4096]{3,2,1,0:T(8,128)(2,1)} %all-gather.10.cloned.1.call-done), kind=kOutput, calls=%fused_computation.27 | convolution fusion | flops 3223977984 | bytes 19922944 | tf_op jit(solution)/shard_map/dot_general | solution.py:32
  264.9 1.3 maximum_bitcast_fusion
  266.1 0.1 copy-done.4
  266.2 1.3 maximum_bitcast_fusion.1
  267.5 0.7 copy-done.2
  268.2 1.4 fusion.13
  269.6 1.3 maximum_bitcast_fusion.2
  270.9 11.0 %all-to-all-done = bf16[192,4,1024]{2,0,1:T(8,128)(2,1)} async-done(((bf16[192,4,1024]{2,0,1:T(8,128)(2,1)}), bf16[192,4,1024]{2,0,1:T(8,128)(2,1)}, u32[]{:S(2)}, u32[]{:S(2)}) %all-to-all-start) | async-done | bytes 1572896 | tf_op jit(solution)/shard_map/all_to_all | solution.py:55
  281.9 25.3 %all-gather.8.cloned.1.call-done = bf16[768,2048]{1,0:T(8,128)(2,1)} async-done(((bf16[192,2048]{1,0:T(8,128)(2,1)}), bf16[768,2048]{1,0:T(8,128)(2,1)}) %all-gather.8.cloned.1.call-update) | async-done | bytes 3145744 | tf_op jit(solution)/shard_map/all_gather | solution.py:56
  307.2 7.8 %convert_bitcast_fusion = bf16[1,1024,2048]{1,2,0:T(8,128)(2,1)} fusion(bf16[768,2048]{1,0:T(8,128)(2,1)} %all-gather.8.cloned.1.call-done, bf16[768,1024]{1,0:T(8,128)(2,1)} %bitcast.18), kind=kOutput, calls=%fused_computation.7 | convolution fusion | flops 3223322624 | bytes 8912896 | tf_op jit(solution)/shard_map/dot_general | solution.py:14
  314.9 6.4 %copy.11 = bf16[1,1024,2048]{2,1,0:T(8,128)(2,1)} copy(bf16[1,1024,2048]{1,2,0:T(8,128)(2,1)} %convert_bitcast_fusion) | data formatting | bytes 8388608
  (18 shorter events, 0.2 us)
Async XLA Ops:
  7.2 111.5 %all-gather.14.cloned.1.call-start = ((), (), s32[]{:S(2)}) async-start(), calls=%async_computation.6 | async-start | bytes 2359296 | tf_op jit(solution)/shard_map/all_gather | solution.py:38
  7.2 39.1 %collective-permute-start.1 = (bf16[1,2,192,2048]{3,2,1,0:T(8,128)(2,1)}, bf16[1,2,192,2048]{3,2,1,0:T(8,128)(2,1)S(1)}, u32[]{:S(2)}, u32[]{:S(2)}) collective-permute-start(bf16[1,2,192,2048]{3,2,1,0:T(8,128)(2,1)} %param.6), channel_id=1, source_target_pairs={{8,0},{16,8},{24,16},{0,24},{9,1},{17,9},{25,17},{1,25},{10,2},{18... | collective-permute-start | bytes 4718600 | tf_op jit(solution)/shard_map/ppermute | solution.py:10
  46.3 1.1 copy-start.5
  48.5 172.1 %all-gather.12.cloned.1.call-start = ((), (), s32[]{:S(2)}) async-start(), calls=%async_computation.5 | async-start | bytes 20971520 | tf_op jit(solution)/shard_map/all_gather | solution.py:27
  49.3 205.5 %all-gather.10.cloned.1.call-start = ((), (), s32[]{:S(2)}) async-start(), calls=%async_computation.4 | async-start | bytes 2359296 | tf_op jit(solution)/shard_map/all_gather | solution.py:31
  49.3 39.8 %collective-permute-start = (bf16[1,2,192,2048]{3,2,1,0:T(8,128)(2,1)}, bf16[1,2,192,2048]{3,2,1,0:T(8,128)(2,1)}, u32[]{:S(2)}, u32[]{:S(2)}) collective-permute-start(bf16[1,2,192,2048]{3,2,1,0:T(8,128)(2,1)} %param.5), channel_id=1, source_target_pairs={{24,0},{0,8},{8,16},{16,24},{25,1},{1,9},{9,17},{17,25},{26,2},{2,... | collective-permute-start | bytes 4718600 | tf_op jit(solution)/shard_map/ppermute | solution.py:10
  49.7 68.9 %collective-permute-start.2 = (bf16[1,2,192,2048]{3,2,1,0:T(8,128)(2,1)}, bf16[1,2,192,2048]{3,2,1,0:T(8,128)(2,1)S(1)}, u32[]{:S(2)}, u32[]{:S(2)}) collective-permute-start(bf16[1,2,192,2048]{3,2,1,0:T(8,128)(2,1)} %param.7), channel_id=1, source_target_pairs={{8,0},{16,8},{24,16},{0,24},{9,1},{17,9},{25,17},{1,25},{10,2},{18... | collective-permute-start | bytes 4718600 | tf_op jit(solution)/shard_map/ppermute | solution.py:10
  91.7 175.8 %reduce-scatter.2.cloned.1.call-start = ((), (), s32[]{:S(2)}) async-start(), calls=%async_computation.2 | async-start | bytes 2359296 | tf_op jit(solution)/shard_map/reduce_scatter | solution.py:50
  118.7 126.8 %copy-start.1 = (bf16[1,2,192,2048]{3,2,1,0:T(8,128)(2,1)}, bf16[1,2,192,2048]{3,2,1,0:T(8,128)(2,1)S(1)}, u32[]{:S(2)}) copy-start(bf16[1,2,192,2048]{3,2,1,0:T(8,128)(2,1)S(1)} %collective-permute-done.2) | copy-start | bytes 4718596
  232.0 12.8 %copy-start.3 = (bf16[192,2048]{1,0:T(8,128)(2,1)}, bf16[192,2048]{1,0:T(8,128)(2,1)S(1)}, u32[]{:S(2)}) copy-start(bf16[192,2048]{1,0:T(8,128)(2,1)S(1)} %get-tuple-element.12) | copy-start | bytes 2359300
  244.9 62.3 %all-gather.8.cloned.1.call-start = ((), (), s32[]{:S(2)}) async-start(), calls=%async_computation.3 | async-start | bytes 3932160 | tf_op jit(solution)/shard_map/all_gather | solution.py:56
  250.2 31.6 %all-to-all-start = ((bf16[192,4,1024]{2,0,1:T(8,128)(2,1)}), bf16[192,4,1024]{2,0,1:T(8,128)(2,1)}, u32[]{:S(2)}, u32[]{:S(2)}) async-start(bf16[192,4,1024]{2,0,1:T(8,128)(2,1)} %copy.10), calls=%async_computation.1 | async-start | bytes 3145728 | tf_op jit(solution)/shard_map/all_to_all | solution.py:55
  254.8 10.0 %copy-start = (bf16[1,192,2048]{2,1,0:T(8,128)(2,1)S(1)}, bf16[1,192,2048]{2,1,0:T(8,128)(2,1)}, u32[]{:S(2)}) copy-start(bf16[1,192,2048]{2,1,0:T(8,128)(2,1)} %get-tuple-element.17) | copy-start | bytes 2359300
  264.8 1.4 copy-start.4
  266.2 2.0 copy-start.2
Sparse Core Ops, SparseCore 0:
  48.7 11.6 all-gather.13
  62.2 158.4 all-gather.11
  222.8 9.7 all-gather.9
  245.0 8.9 reduce-scatter.1
  255.7 51.4 all-gather.7
where the time goes:
time: 329 us; the launch traced here: 328 us
  waiting for transfers between devices  235 us (71%)
  matrix products  42 us (13%)
  local copies, waits for them, and re-layouts  16.5 us (5%)
  between operations  14.5 us (4%)
  starting transfers between devices  14.2 us (4%)
  other arithmetic  5.4 us (2%)
    all_gather x1, waiting for transfers between devices, local(): whole_weight = lax.all_gather(local_weight, 'dp', axis=0, tiled=True)  102 us
    ppermute x3, waiting for transfers between devices, shifted(): return lax.ppermute(block, axis, route)  95.8 us
    all_gather x1, waiting for transfers between devices, local(): hidden_all = lax.all_gather(hidden, 'dp', axis=0, tiled=True)  25.3 us
    dot_general x1, matrix products, local(): lax.dot_general(hidden, whole_weight, (((1,), (1,)), ((), ())), preferred...  12.8 us
    dot_general x1, matrix products, local(): jnp.dot(lower_full, whole_weight, preferred_element_type=jnp.float32)  11.4 us
    all_to_all x1, waiting for transfers between devices, local(): lax.all_to_all(lower_full, 'dp', split_axis=1, concat_axis=0, tiled=True)  11 us
    dot_general x1, matrix products, local(): pre = jnp.dot(upper_full, whole_weight, preferred_element_type=jnp.float32)  9.98 us
    ppermute x3, starting transfers between devices, shifted(): return lax.ppermute(block, axis, route)  9.43 us
  transfers between devices with their start and end apart: 9, of which 6 were waited for; matrix products, arithmetic and copies ran while one was open for 13% of the time, Pallas kernels for 0%

commit v1 on v0

v1 whole, which is shorter than its diff:
```python
import jax
import jax.numpy as jnp
from jax import lax
from jax.sharding import PartitionSpec as P


def shifted(block, axis, distance):
    devices = range(lax.axis_size(axis))
    route = [((i - distance) % len(devices), i) for i in devices]
    return lax.ppermute(block, axis, route)


def across_rows(left, right):
    return lax.dot_general(
        left, right, (((0,), (0,)), ((), ())), preferred_element_type=jnp.float32
    )


def slope(hidden):
    sigma = jax.nn.sigmoid(hidden)
    return sigma * (1.0 + hidden * (1.0 - sigma))


def local(sent_out, sent_back, sent_grad, lengths, weight):
    token_rows = sent_out.shape[2]
    own_weight = weight[0]

    def shares(block):
        full = lax.all_gather(block, "tensor", axis=1, tiled=True)
        return lax.all_to_all(full, "dp", split_axis=1, concat_axis=0, tiled=True)

    def project(share):
        partial = jnp.dot(share, own_weight, preferred_element_type=jnp.float32)
        return lax.psum_scatter(
            partial.astype(jnp.bfloat16), "dp", scatter_dimension=0, tiled=True
        ).astype(jnp.float32)

    back_lower = shifted(sent_back[0, 1], "section", -1)
    upper_in = shifted(sent_out[0, 0], "section", 1)
    incoming_upper = shifted(sent_grad[0, 0], "section", -1)
    lower_in = shifted(sent_out[0, 1], "section", 1)
    back_upper = shifted(sent_back[0, 0], "section", -1)
    incoming_lower = shifted(sent_grad[0, 1], "section", -1)

    held_share = shares(back_lower)
    pre_held = project(held_share)
    keep = (jnp.arange(token_rows, dtype=jnp.int32) < lengths[0, 0])[:, None]
    zero = jnp.zeros((), jnp.bfloat16)
    dupper = jnp.where(keep, incoming_upper, zero)
    dlower = jnp.where(keep, incoming_lower, zero)
    hidden = (dupper.astype(jnp.float32) * slope(pre_held)).astype(jnp.bfloat16)
    hidden_all = lax.all_gather(hidden, "dp", axis=0, tiled=True)
    rebuilt_lower = (back_upper.astype(jnp.float32) - jax.nn.silu(pre_held)).astype(jnp.bfloat16)
    rebuilt = jnp.stack([back_lower, rebuilt_lower])[None]

    pre = project(shares(upper_in))
    upper_out = (lower_in.astype(jnp.float32) + jax.nn.silu(pre)).astype(jnp.bfloat16)
    emitted = jnp.stack([upper_out, upper_in])[None]

    terms = lax.dot_general(
        hidden_all, own_weight, (((1,), (1,)), ((), ())), preferred_element_type=jnp.float32
    ).astype(jnp.bfloat16)
    terms = lax.all_to_all(terms, "dp", split_axis=0, concat_axis=1, tiled=True)
    through = lax.psum_scatter(terms, "tensor", scatter_dimension=1, tiled=True).astype(jnp.float32)
    dupper_in = (dlower.astype(jnp.float32) + through).astype(jnp.bfloat16)
    grads_out = jnp.stack([dupper_in, dupper])[None]
    weight_grad = across_rows(held_share, hidden_all).astype(jnp.bfloat16)[None]
    return (emitted, rebuilt, grads_out, weight_grad)


def solution(mesh):
    return jax.shard_map(
        local,
        mesh=mesh,
        in_specs=(
            P("section", None, "dp", "tensor"),
            P("section", None, "dp", "tensor"),
            P("section", None, "dp", "tensor"),
            P("section", "dp"),
            P("section", "dp", "tensor"),
        ),
        out_specs=(
            P("section", None, "dp", "tensor"),
            P("section", None, "dp", "tensor"),
            P("section", None, "dp", "tensor"),
            P("section", "dp", "tensor"),
        ),
        check_vma=False,
    )
```

time: 329 us -> 289 us (0.88)
  waiting for transfers between devices: 235 us -> 117 us
  blocking collectives: 0 us -> 91.6 us
  matrix products: 42 us -> 21.1 us
  local copies, waits for them, and re-layouts: 16.5 us -> 21.4 us
  other arithmetic: 5.4 us -> 10.2 us
    all_to_all x0 -> x3, blocking collectives: none -> 91.6 us  [the longest x2 52.7 us: shares(): return lax.all_to_all(full, 'dp', split_axis=1, concat_axis=0, tiled=True)]
    all_gather x3 -> x2, waiting for transfers between devices: 102 us -> 11.8 us  [shares(): full = lax.all_gather(block, 'tensor', axis=1, tiled=True)]
    dot_general x3, matrix products: 34.2 us -> 16.1 us  [the longest x2 9.48 us: project(): partial = jnp.dot(share, own_weight, preferred_element_type=jnp.float32)]
    all_to_all x1 -> x0, waiting for transfers between devices: 11 us -> none  [local(): lax.all_to_all(lower_full, 'dp', split_axis=1, concat_axis=0, tiled=True)]
    ppermute x3 -> x6, waiting for transfers between devices: 95.8 us -> 85.4 us  [shifted(): return lax.ppermute(block, axis, route)]
    all_gather x1, waiting for transfers between devices: 25.3 us -> 19.6 us  [local(): hidden_all = lax.all_gather(hidden, 'dp', axis=0, tiled=True)]
    all_to_all x1 -> x0, starting transfers between devices: 4.55 us -> none  [local(): lax.all_to_all(lower_full, 'dp', split_axis=1, concat_axis=0, tiled=True)]
    squeeze x0 -> x3, local copies, waits for them, and re-layouts: none -> 4.41 us  [the longest x1 2.43 us: local(): back_upper = shifted(sent_back[0, 0], 'section', -1)]
  transfers between devices with their start and end apart: 9 -> 12, of which waited for: 6 -> 7; matrix products, arithmetic and copies ran while one was open for 13% -> 12% of each run, Pallas kernels for 0% -> 0%
where the time goes in v1:
time: 289 us
  waiting for transfers between devices  117 us (40%)
  blocking collectives  91.6 us (32%)
  local copies, waits for them, and re-layouts  21.4 us (7%)
  matrix products  21.1 us (7%)
  between operations  14.9 us (5%)
  starting transfers between devices  12.8 us (4%)
  other arithmetic  10.2 us (4%)
    ppermute x6, waiting for transfers between devices, shifted(): return lax.ppermute(block, axis, route)  85.4 us
    all_to_all x2, blocking collectives, shares(): return lax.all_to_all(full, 'dp', split_axis=1, concat_axis=0, tiled=True)  52.7 us
    all_to_all x1, blocking collectives, local(): terms = lax.all_to_all(terms, 'dp', split_axis=0, concat_axis=1, tiled=True)  38.9 us
    all_gather x1, waiting for transfers between devices, local(): hidden_all = lax.all_gather(hidden, 'dp', axis=0, tiled=True)  19.6 us
    ppermute x6, starting transfers between devices, shifted(): return lax.ppermute(block, axis, route)  12.5 us
    unnamed x25, local copies, waits for them, and re-layouts  12.3 us
    all_gather x2, waiting for transfers between devices, shares(): full = lax.all_gather(block, 'tensor', axis=1, tiled=True)  11.8 us
    dot_general x2, matrix products, project(): partial = jnp.dot(share, own_weight, preferred_element_type=jnp.float32)  9.48 us
  transfers between devices with their start and end apart: 12, of which 7 were waited for; matrix products, arithmetic and copies ran while one was open for 12% of the time, Pallas kernels for 0%

profile of v1, /device:TPU:0, one launch (start us, length us, event | category | flops | bytes accessed | tf_op | source)
XLA Modules:
  0.0 288.8 jit_solution(7391464849257525765)
XLA Ops:
  7.2 2.4 slice_bitcast_fusion.2
  9.6 5.1 %collective-permute-start.2 = (bf16[192,2048]{1,0:T(8,128)(2,1)S(1)}, bf16[192,2048]{1,0:T(8,128)(2,1)S(1)}, u32[]{:S(2)}, u32[]{:S(2)}) collective-permute-start(bf16[192,2048]{1,0:T(8,128)(2,1)S(1)} %get-tuple-element.19), channel_id=1, source_target_pairs={{8,0},{16,8},{24,16},{0,24},{9,1},{17,9},{25,17},{1,25},{10,2},{18... | collective-permute-start | bytes 2359304 | tf_op jit(solution)/shard_map/ppermute | solution.py:10
  14.7 16.8 %collective-permute-done.2 = bf16[192,2048]{1,0:T(8,128)(2,1)S(1)} collective-permute-done((bf16[192,2048]{1,0:T(8,128)(2,1)S(1)}, bf16[192,2048]{1,0:T(8,128)(2,1)S(1)}, u32[]{:S(2)}, u32[]{:S(2)}) %collective-permute-start.2) | collective-permute-done | bytes 786464 | tf_op jit(solution)/shard_map/ppermute | solution.py:10
  32.5 11.8 %all-gather.6.cloned.1.call-done = bf16[192,4096]{1,0:T(8,128)(2,1)} async-done(((bf16[192,2048]{1,0:T(8,128)(2,1)}), bf16[192,4096]{1,0:T(8,128)(2,1)}) %all-gather.6.cloned.1.call-update) | async-done | bytes 1572880 | tf_op jit(solution)/shard_map/all_gather | solution.py:29
  44.3 1.7 copy.24
  46.0 24.1 %all_to_all.57 = bf16[192,4,1024]{2,0,1:T(8,128)(2,1)S(1)} all-to-all(bf16[192,4,1024]{2,0,1:T(8,128)(2,1)S(1)} %bitcast.71), channel_id=1, replica_groups=mesh['section'=4,'dp'=4,'tensor'=2] {'dp'}, dimensions={1} | all-to-all | bytes 3145728 | tf_op jit(solution)/shard_map/all_to_all | solution.py:30
  70.1 1.2 copy-done.6
  71.3 4.7 %fusion.9 = bf16[768,2048]{1,0:T(8,128)(2,1)} fusion(bf16[768,1024]{1,0:T(8,128)(2,1)S(1)} %bitcast.76, bf16[1,1024,2048]{2,1,0:T(8,128)(2,1)S(1)} %copy-done.9), kind=kOutput, calls=%fused_computation.8 | convolution fusion | flops 3222798336 | bytes 8912896 | tf_op jit(solution)/shard_map/dot_general | solution.py:33
  76.1 1.3 copy-done.4
  78.4 1.5 collective-permute-start.1
  79.9 18.6 %collective-permute-done.1 = bf16[192,2048]{1,0:T(8,128)(2,1)S(1)} collective-permute-done((bf16[192,2048]{1,0:T(8,128)(2,1)S(1)}, bf16[192,2048]{1,0:T(8,128)(2,1)S(1)}, u32[]{:S(2)}, u32[]{:S(2)}) %collective-permute-start.1) | collective-permute-done | bytes 786464 | tf_op jit(solution)/shard_map/ppermute | solution.py:10
  100.4 1.5 collective-permute-start.5
  103.2 17.7 %collective-permute-done.5 = bf16[192,2048]{1,0:T(8,128)(2,1)S(1)} collective-permute-done((bf16[192,2048]{1,0:T(8,128)(2,1)S(1)}, bf16[192,2048]{1,0:T(8,128)(2,1)S(1)}, u32[]{:S(2)}, u32[]{:S(2)}) %collective-permute-start.5) | collective-permute-done | bytes 786464 | tf_op jit(solution)/shard_map/ppermute | solution.py:10
  120.8 13.8 %collective-permute-done.3 = bf16[192,2048]{1,0:T(8,128)(2,1)S(1)} collective-permute-done((bf16[192,2048]{1,0:T(8,128)(2,1)S(1)}, bf16[192,2048]{1,0:T(8,128)(2,1)S(1)}, u32[]{:S(2)}, u32[]{:S(2)}) %collective-permute-start.3) | collective-permute-done | bytes 786464 | tf_op jit(solution)/shard_map/ppermute | solution.py:10
  134.7 2.9 fusion.27
  137.7 1.7 copy.25
  139.4 28.6 %all_to_all.58 = bf16[192,4,1024]{2,0,1:T(8,128)(2,1)S(1)} all-to-all(bf16[192,4,1024]{2,0,1:T(8,128)(2,1)S(1)} %bitcast.72), channel_id=1, replica_groups=mesh['section'=4,'dp'=4,'tensor'=2] {'dp'}, dimensions={1} | all-to-all | bytes 3145728 | tf_op jit(solution)/shard_map/all_to_all | solution.py:30
  168.0 4.7 %fusion.6 = bf16[768,2048]{1,0:T(8,128)(2,1)} fusion(bf16[768,1024]{1,0:T(8,128)(2,1)S(1)} %bitcast.80, bf16[1,1024,2048]{2,1,0:T(8,128)(2,1)S(1)} %copy-done.10), kind=kOutput, calls=%fused_computation.7 | convolution fusion | flops 3222798336 | bytes 8912896 | tf_op jit(solution)/shard_map/dot_general | solution.py:33
  172.8 19.6 %all-gather.8.cloned.1.call-done = bf16[768,2048]{1,0:T(8,128)(2,1)} async-done(((bf16[192,2048]{1,0:T(8,128)(2,1)}), bf16[768,2048]{1,0:T(8,128)(2,1)}) %all-gather.8.cloned.1.call-update) | async-done | bytes 3145744 | tf_op jit(solution)/shard_map/all_gather | solution.py:52
  192.4 6.6 %fusion.12 = bf16[768,1024]{1,0:T(8,128)(2,1)S(1)} fusion(bf16[768,2048]{1,0:T(8,128)(2,1)} %all-gather.8.cloned.1.call-done, bf16[1,1024,2048]{2,1,0:T(8,128)(2,1)} %param.9), kind=kOutput, calls=%fused_computation.14 | convolution fusion | flops 3222011904 | bytes 8912896 | tf_op jit(solution)/shard_map/dot_general | solution.py:60
  199.0 38.9 %all_to_all.59 = bf16[4,192,1024]{2,1,0:T(8,128)(2,1)S(1)} all-to-all(bf16[4,192,1024]{2,1,0:T(8,128)(2,1)S(1)} %bitcast.81), channel_id=1, replica_groups=mesh['section'=4,'dp'=4,'tensor'=2] {'dp'}, dimensions={0} | all-to-all | bytes 3145728 | tf_op jit(solution)/shard_map/all_to_all | solution.py:63
  237.9 1.3 copy.21
  239.2 1.5 collective-permute-start
  240.7 2.3 collective-permute-start.4
  243.2 18.6 %collective-permute-done = bf16[192,2048]{1,0:T(8,128)(2,1)} collective-permute-done((bf16[192,2048]{1,0:T(8,128)(2,1)}, bf16[192,2048]{1,0:T(8,128)(2,1)}, u32[]{:S(2)}, u32[]{:S(2)}) %collective-permute-start) | collective-permute-done | bytes 786464 | tf_op jit(solution)/shard_map/ppermute | solution.py:10
  261.8 1.9 fusion.30
  263.7 1.3 maximum_bitcast_fusion
  265.1 1.3 maximum_bitcast_fusion.1
  267.8 5.0 %convert_bitcast_fusion = bf16[1,1024,2048]{1,2,0:T(8,128)(2,1)} fusion(bf16[768,2048]{1,0:T(8,128)(2,1)S(1)} %copy-done.11, bf16[768,1024]{1,0:T(8,128)(2,1)S(1)} %bitcast.77), kind=kOutput, calls=%fused_computation.6 | convolution fusion | flops 3223322624 | bytes 8912896 | tf_op jit(solution)/shard_map/dot_general | solution.py:14
  272.8 6.4 %copy.18 = bf16[1,1024,2048]{2,1,0:T(8,128)(2,1)} copy(bf16[1,1024,2048]{1,2,0:T(8,128)(2,1)} %convert_bitcast_fusion) | data formatting | bytes 8388608
  279.2 1.4 fusion.29
  280.6 1.3 maximum_bitcast_fusion.2
  (44 shorter events, 6.4 us)
Async XLA Ops:
  7.2 37.2 %all-gather.6.cloned.1.call-start = ((), (), s32[]{:S(2)}) async-start(), calls=%async_computation.8 | async-start | bytes 2359296 | tf_op jit(solution)/shard_map/all_gather | solution.py:29
  9.6 21.9 %collective-permute-start.2 = (bf16[192,2048]{1,0:T(8,128)(2,1)S(1)}, bf16[192,2048]{1,0:T(8,128)(2,1)S(1)}, u32[]{:S(2)}, u32[]{:S(2)}) collective-permute-start(bf16[192,2048]{1,0:T(8,128)(2,1)S(1)} %get-tuple-element.19), channel_id=1, source_target_pairs={{8,0},{16,8},{24,16},{0,24},{9,1},{17,9},{25,17},{1,25},{10,2},{18... | collective-permute-start | bytes 2359304 | tf_op jit(solution)/shard_map/ppermute | solution.py:10
  31.5 0.9 copy-start
  32.4 102.2 %reduce-scatter.6.cloned.1.call-start = ((), (), s32[]{:S(2)}) async-start(), calls=%async_computation.9 | async-start | bytes 3932160 | tf_op jit(solution)/shard_map/reduce_scatter | solution.py:34
  44.3 26.9 %copy-start.9 = (bf16[1,1024,2048]{2,1,0:T(8,128)(2,1)S(1)}, bf16[1,1024,2048]{2,1,0:T(8,128)(2,1)}, u32[]{:S(2)}) copy-start(bf16[1,1024,2048]{2,1,0:T(8,128)(2,1)} %param.9) | copy-start | bytes 12582916
  70.1 1.2 copy-start.6
  76.0 1.4 copy-start.4
  76.0 23.4 %copy-start.5 = (bf16[1,2,192,2048]{3,2,1,0:T(8,128)(2,1)S(1)}, bf16[1,2,192,2048]{3,2,1,0:T(8,128)(2,1)}, u32[]{:S(2)}) copy-start(bf16[1,2,192,2048]{3,2,1,0:T(8,128)(2,1)} %param.7) | copy-start | bytes 4718596
  76.0 61.6 %all-gather.4.cloned.1.call-start = ((), (), s32[]{:S(2)}) async-start(), calls=%async_computation.6 | async-start | bytes 2359296 | tf_op jit(solution)/shard_map/all_gather | solution.py:29
  78.4 20.0 %collective-permute-start.1 = (bf16[192,2048]{1,0:T(8,128)(2,1)S(1)}, bf16[192,2048]{1,0:T(8,128)(2,1)S(1)}, u32[]{:S(2)}, u32[]{:S(2)}) collective-permute-start(bf16[192,2048]{1,0:T(8,128)(2,1)S(1)} %get-tuple-element.21), channel_id=1, source_target_pairs={{24,0},{0,8},{8,16},{16,24},{25,1},{1,9},{9,17},{17,25},{26,2},{2,... | collective-permute-start | bytes 2359304 | tf_op jit(solution)/shard_map/ppermute | solution.py:10
  98.5 0.9 copy-start.2
  99.4 2.6 copy-start.8
  99.4 93.0 %all-gather.8.cloned.1.call-start = ((), (), s32[]{:S(2)}) async-start(), calls=%async_computation.10 | async-start | bytes 3932160 | tf_op jit(solution)/shard_map/all_gather | solution.py:52
  100.4 20.4 %collective-permute-start.5 = (bf16[192,2048]{1,0:T(8,128)(2,1)S(1)}, bf16[192,2048]{1,0:T(8,128)(2,1)S(1)}, u32[]{:S(2)}, u32[]{:S(2)}) collective-permute-start(bf16[192,2048]{1,0:T(8,128)(2,1)S(1)} %get-tuple-element.17), channel_id=1, source_target_pairs={{8,0},{16,8},{24,16},{0,24},{9,1},{17,9},{25,17},{1,25},{10,2},{18... | collective-permute-start | bytes 2359304 | tf_op jit(solution)/shard_map/ppermute | solution.py:10
  102.0 32.7 %collective-permute-start.3 = (bf16[192,2048]{1,0:T(8,128)(2,1)S(1)}, bf16[192,2048]{1,0:T(8,128)(2,1)S(1)}, u32[]{:S(2)}, u32[]{:S(2)}) collective-permute-start(bf16[192,2048]{1,0:T(8,128)(2,1)S(1)} %copy-done.8), channel_id=1, source_target_pairs={{8,0},{16,8},{24,16},{0,24},{9,1},{17,9},{25,17},{1,25},{10,2},{18... | collective-permute-start | bytes 2359304 | tf_op jit(solution)/shard_map/ppermute | solution.py:10
  137.6 124.2 %reduce-scatter.4.cloned.1.call-start = ((), (), s32[]{:S(2)}) async-start(), calls=%async_computation.7 | async-start | bytes 3932160 | tf_op jit(solution)/shard_map/reduce_scatter | solution.py:34
  137.7 30.3 %copy-start.10 = (bf16[1,1024,2048]{2,1,0:T(8,128)(2,1)S(1)}, bf16[1,1024,2048]{2,1,0:T(8,128)(2,1)}, u32[]{:S(2)}) copy-start(bf16[1,1024,2048]{2,1,0:T(8,128)(2,1)} %param.9) | copy-start | bytes 12582916
  172.8 106.4 %reduce-scatter.8.cloned.1.call-start = ((), (), s32[]{:S(2)}) async-start(), calls=%async_computation.11 | async-start | bytes 2359296 | tf_op jit(solution)/shard_map/reduce_scatter | solution.py:64
  239.2 22.6 %collective-permute-start = (bf16[192,2048]{1,0:T(8,128)(2,1)}, bf16[192,2048]{1,0:T(8,128)(2,1)}, u32[]{:S(2)}, u32[]{:S(2)}) collective-permute-start(bf16[192,2048]{1,0:T(8,128)(2,1)} %get-tuple-element.20), channel_id=1, source_target_pairs={{24,0},{0,8},{8,16},{16,24},{25,1},{1,9},{9,17},{17,25},{26,2},{2,... | collective-permute-start | bytes 2359304 | tf_op jit(solution)/shard_map/ppermute | solution.py:10
  240.7 38.5 %collective-permute-start.4 = (bf16[192,2048]{1,0:T(8,128)(2,1)}, bf16[192,2048]{1,0:T(8,128)(2,1)S(1)}, u32[]{:S(2)}, u32[]{:S(2)}) collective-permute-start(bf16[192,2048]{1,0:T(8,128)(2,1)} %get-tuple-element.16), channel_id=1, source_target_pairs={{8,0},{16,8},{24,16},{0,24},{9,1},{17,9},{25,17},{1,25},{10,2},{18... | collective-permute-start | bytes 2359304 | tf_op jit(solution)/shard_map/ppermute | solution.py:10
  243.2 20.5 %copy-start.3 = (bf16[192,2048]{1,0:T(8,128)(2,1)S(1)}, bf16[192,2048]{1,0:T(8,128)(2,1)}, u32[]{:S(2)}) copy-start(bf16[192,2048]{1,0:T(8,128)(2,1)} %copy-done.2) | copy-start | bytes 2359300
  263.7 1.5 copy-start.1
  263.7 3.4 %copy-start.11 = (bf16[768,2048]{1,0:T(8,128)(2,1)S(1)}, bf16[768,2048]{1,0:T(8,128)(2,1)}, u32[]{:S(2)}) copy-start(bf16[768,2048]{1,0:T(8,128)(2,1)} %all-gather.8.cloned.1.call-done) | copy-start | bytes 9437188
  265.1 2.7 copy-start.7
Sparse Core Ops, SparseCore 0:
  32.6 11.7 all-gather.5
  76.2 43.3 reduce-scatter.5
  121.7 9.7 all-gather.3
  137.7 54.6 all-gather.7
  195.8 60.2 reduce-scatter.3
  258.8 8.9 reduce-scatter.7

commit v2 on v1

--- a/solution.py
+++ b/solution.py
@@ -1,6 +1,10 @@
+import functools
+
 import jax
 import jax.numpy as jnp
 from jax import lax
+from jax.experimental import pallas as pl
+from jax.experimental.pallas import tpu as pltpu
 from jax.sharding import PartitionSpec as P
 
 
@@ -21,7 +25,7 @@
     return sigma * (1.0 + hidden * (1.0 - sigma))
 
 
-def local(sent_out, sent_back, sent_grad, lengths, weight):
+def spread(sent_out, sent_back, sent_grad, lengths, weight):
     token_rows = sent_out.shape[2]
     own_weight = weight[0]
 
@@ -68,9 +72,344 @@
     return (emitted, rebuilt, grads_out, weight_grad)
 
 
+MESH = pl.DeviceIdType.MESH
+BACK_LOWER, GRAD_UPPER, BACK_UPPER, GRAD_LOWER, OUT_UPPER, OUT_LOWER = range(6)
+
+
+def step_kernel(
+    lengths, sent_out, sent_back, sent_grad, weight,
+    emitted, rebuilt, grads_out, weight_grad,
+    w, got, share, part, summed, hidden, terms, tx, trx, ts, tr, stage, wg,
+    z_send, z_recv, d_send, d_recv, r_send, r_recv, p_send, p_recv,
+    h_send, h_recv, t_send, t_recv, f_send, f_recv, w_sem, o_sem,
+):
+    f32, bf16 = jnp.float32, jnp.bfloat16
+    n_s, n_d, n_t = (lax.axis_size(a) for a in ("section", "dp", "tensor"))
+    me_s, me_d, me_t = (lax.axis_index(a) for a in ("section", "dp", "tensor"))
+    rows, local_features = got.shape[1], got.shape[2]
+    half, depth = share.shape[3], share.shape[4]
+    per = local_features // depth
+    other = 1 - me_t
+    nxt, prv = lax.rem(me_s + 1, n_s), lax.rem(me_s + n_s - 1, n_s)
+
+    def replica(k):
+        return lax.rem(me_d + k + n_d, n_d)
+
+    barrier = pltpu.get_barrier_semaphore()
+    for k in range(n_d):
+        for c in range(n_t):
+            if k or c:
+                pl.semaphore_signal(
+                    barrier, inc=1, device_id=(me_s, replica(k), lax.rem(me_t + c, n_t)), device_id_type=MESH
+                )
+    for z in (nxt, prv):
+        pl.semaphore_signal(barrier, inc=1, device_id=(z, me_d, me_t), device_id_type=MESH)
+    pl.semaphore_wait(barrier, n_d * n_t - 1 + 2)
+
+    def remote(src, dst, send, recv, where):
+        return pltpu.make_async_remote_copy(
+            src_ref=src, dst_ref=dst, send_sem=send, recv_sem=recv, device_id=where, device_id_type=MESH
+        )
+
+    def landed(dst, sem):
+        pltpu.make_async_copy(dst, dst, sem).wait()
+
+    def along_z(i):
+        src, piece, z = {
+            BACK_LOWER: (sent_back, 1, prv), BACK_UPPER: (sent_back, 0, prv),
+            GRAD_UPPER: (sent_grad, 0, prv), GRAD_LOWER: (sent_grad, 1, prv),
+            OUT_UPPER: (sent_out, 0, nxt), OUT_LOWER: (sent_out, 1, nxt),
+        }[i]
+        return remote(src.at[0, piece], got.at[i], z_send.at[i], z_recv.at[i], (z, me_d, me_t))
+
+    along_z(BACK_LOWER).start()
+    w_copy = pltpu.make_async_copy(weight.at[0], w, w_sem)
+    w_copy.start()
+    along_z(GRAD_UPPER).start()
+    along_z(BACK_UPPER).start()
+    along_z(GRAD_LOWER).start()
+
+    def deal(i, x, finish):
+        for h in range(n_t):
+            for j in range(per):
+                n = h * per + j
+                target = me_t * per + j
+                src = got.at[i, pl.ds(h * half, half), pl.ds(j * depth, depth)]
+                dst = share.at[x, me_d, h]
+                own = jnp.logical_and(target == me_d, me_t == h)
+
+                @pl.when(own)
+                def _():
+                    if not finish:
+                        pltpu.make_async_copy(src, dst, d_recv.at[x, me_d]).start()
+
+                @pl.when(jnp.logical_not(own))
+                def _():
+                    copy = remote(src, dst, d_send.at[x, n], d_recv.at[x, me_d], (me_s, target, h))
+                    if finish:
+                        copy.wait_send()
+                    else:
+                        copy.start()
+
+    def relay(x, k):
+        r = replica(k)
+        return remote(
+            share.at[x, r, me_t], share.at[x, r, me_t], r_send.at[x, r], r_recv.at[x, r], (me_s, me_d, other)
+        )
+
+    def partial(x, k):
+        r = replica(k)
+        return remote(
+            part.at[x, r], summed.at[x, k - 1], p_send.at[x, k - 1], p_recv.at[x, k - 1], (me_s, r, me_t)
+        )
+
+    def gather(x):
+        for k in range(n_d):
+            landed(share.at[x, replica(k), me_t], d_recv.at[x, replica(k)])
+            relay(x, k).start()
+        for k in range(n_d):
+            landed(share.at[x, replica(k), other], r_recv.at[x, replica(k)])
+
+    def multiply(x, send):
+        for k in list(range(1, n_d)) + [0]:
+            r = replica(k)
+
+            @pl.loop(0, local_features // 512)
+            def _(c):
+                cols = pl.ds(pl.multiple_of(c * 512, 512), 512)
+                left = share[x, r].reshape(rows, depth)
+                part[x, r, :, cols] = jnp.dot(left, w[:, cols], preferred_element_type=f32).astype(bf16)
+
+            if send and k:
+                partial(x, k).start()
+
+    def total(x, cols):
+        pre = part[x, me_d, :, cols].astype(f32)
+        for k in range(n_d - 1):
+            pre = pre + summed[x, k, :, cols].astype(f32)
+        return pre
+
+    def tiles(body):
+        @pl.loop(0, local_features // 256)
+        def _(c):
+            body(pl.ds(pl.multiple_of(c * 256, 256), 256))
+
+    def out(i, src, dst):
+        return pltpu.make_async_copy(src, dst, o_sem.at[i])
+
+    outs = [
+        out(0, got.at[BACK_LOWER], rebuilt.at[0, 0]),
+        out(1, got.at[OUT_UPPER], emitted.at[0, 1]),
+        out(2, stage.at[0], grads_out.at[0, 1]),
+        out(3, stage.at[1], rebuilt.at[0, 1]),
+        out(4, stage.at[2], emitted.at[0, 0]),
+        out(5, stage.at[3], grads_out.at[0, 0]),
+        out(6, wg, weight_grad.at[0]),
+    ]
+
+    along_z(BACK_LOWER).wait_recv()
+    along_z(OUT_UPPER).start()
+    deal(BACK_LOWER, 0, False)
+    outs[0].start()
+    gather(0)
+    w_copy.wait()
+    multiply(0, True)
+
+    along_z(OUT_UPPER).wait_recv()
+    along_z(OUT_LOWER).start()
+    deal(OUT_UPPER, 1, False)
+    outs[1].start()
+    gather(1)
+    multiply(1, False)
+
+    along_z(GRAD_UPPER).wait_recv()
+    for k in range(1, n_d):
+        partial(0, k).wait_recv()
+    live = lengths[0, 0]
+
+    def keep(block):
+        place = lax.broadcasted_iota(jnp.int32, block.shape, 0)
+        return jnp.where(place < live, block.astype(f32), 0.0)
+
+    def hide(cols):
+        pre = total(0, cols)
+        dupper = keep(got[GRAD_UPPER, :, cols])
+        stage[0, :, cols] = dupper.astype(bf16)
+        sigma = jax.nn.sigmoid(pre)
+        gated = (dupper * (sigma * (1.0 + pre * (1.0 - sigma)))).astype(bf16)
+        hidden[me_d, :, :, cols] = gated.reshape(n_t, half, 256)
+
+    tiles(hide)
+
+    def show(k):
+        return remote(
+            hidden.at[me_d], hidden.at[me_d], h_send.at[k - 1], h_recv.at[k - 1], (me_s, replica(k), me_t)
+        )
+
+    for k in range(1, n_d):
+        show(k).start()
+    for k in range(1, n_d):
+        partial(1, k).start()
+    outs[2].start()
+
+    along_z(BACK_UPPER).wait_recv()
+
+    def rebuild(cols):
+        pre = total(0, cols)
+        upper = got[BACK_UPPER, :, cols].astype(f32)
+        stage[1, :, cols] = (upper - pre * jax.nn.sigmoid(pre)).astype(bf16)
+
+    tiles(rebuild)
+    outs[3].start()
+
+    for k in range(1, n_d):
+        landed(hidden.at[replica(-k)], h_recv.at[k - 1])
+
+    @pl.loop(0, depth // 256)
+    def _(c):
+        cols = pl.ds(pl.multiple_of(c * 256, 256), 256)
+        left = hidden[...].reshape(n_d * rows, local_features)
+        product = lax.dot_general(left, w[cols, :], (((1,), (1,)), ((), ())), preferred_element_type=f32)
+        terms[:, :, :, cols] = product.reshape(n_d, n_t, half, 256)
+
+    for r in range(n_d):
+        tx[r] = terms[r, other].astype(bf16)
+    swap = remote(tx, trx, t_send, t_recv, (me_s, me_d, other))
+    swap.start()
+
+    def weigh(lo, hi):
+        @pl.loop(lo, hi)
+        def _(c):
+            cols = pl.ds(pl.multiple_of(c * 256, 256), 256)
+            left = share[0, :, :, :, cols].reshape(n_d * rows, 256)
+            right = hidden[...].reshape(n_d * rows, local_features)
+            product = lax.dot_general(left, right, (((0,), (0,)), ((), ())), preferred_element_type=f32)
+            wg[cols, :] = product.astype(bf16)
+
+    swap.wait_recv()
+    owner, place = lax.div(me_d, per), lax.rem(me_d, per)
+
+    def back_to(k, finish):
+        r = replica(k)
+        src, dst = ts.at[r], tr.at[place, me_t]
+        own = jnp.logical_and(k == 0, me_t == owner)
+
+        @pl.when(own)
+        def _():
+            if not finish:
+                pltpu.make_async_copy(src, dst, f_recv.at[place, me_t]).start()
+
+        @pl.when(jnp.logical_not(own))
+        def _():
+            copy = remote(src, dst, f_send.at[k], f_recv.at[place, me_t], (me_s, r, owner))
+            if finish:
+                copy.wait_send()
+            else:
+                copy.start()
+
+    for k in range(1, n_d + 1):
+        r = replica(k)
+        ts[r] = (terms[r, me_t] + trx[r].astype(f32)).astype(bf16)
+        back_to(k % n_d, False)
+
+    weigh(0, depth // 256)
+    outs[6].start()
+
+    along_z(OUT_LOWER).wait_recv()
+    for k in range(1, n_d):
+        partial(1, k).wait_recv()
+
+    def emit(cols):
+        pre = total(1, cols)
+        lower = got[OUT_LOWER, :, cols].astype(f32)
+        stage[2, :, cols] = (lower + pre * jax.nn.sigmoid(pre)).astype(bf16)
+
+    tiles(emit)
+    outs[4].start()
+
+    along_z(GRAD_LOWER).wait_recv()
+    for j in range(per):
+        for h in range(n_t):
+            landed(tr.at[j, h], f_recv.at[j, h])
+
+    for j in range(per):
+        span = pl.ds(j * depth, depth)
+        through = tr[j].reshape(rows, depth).astype(f32)
+        stage[3, :, span] = (keep(got[GRAD_LOWER, :, span]) + through).astype(bf16)
+    outs[5].start()
+
+    for i in range(6):
+        along_z(i).wait_send()
+    for x, i in ((0, BACK_LOWER), (1, OUT_UPPER)):
+        deal(i, x, True)
+        for k in range(n_d):
+            relay(x, k).wait_send()
+        for k in range(1, n_d):
+            partial(x, k).wait_send()
+    for k in range(1, n_d):
+        show(k).wait_send()
+    swap.wait_send()
+    for k in range(n_d):
+        back_to(k, True)
+    for copy in outs:
+        copy.wait()
+
+
+def together(sizes, sent_out, sent_back, sent_grad, lengths, weight):
+    n_d, n_t = sizes
+    rows, features = sent_out.shape[2:]
+    depth = weight.shape[1]
+    half, per = rows // n_t, features // depth
+    bf16 = jnp.bfloat16
+    dma, vmem = pltpu.SemaphoreType.DMA, pltpu.VMEM
+    anywhere = pl.BlockSpec(memory_space=pl.ANY)
+    return pl.pallas_call(
+        step_kernel,
+        out_shape=[jax.ShapeDtypeStruct(a.shape, bf16) for a in (sent_out, sent_back, sent_grad, weight)],
+        in_specs=[pl.BlockSpec(memory_space=pltpu.SMEM)] + [anywhere] * 4,
+        out_specs=[anywhere] * 4,
+        scratch_shapes=[
+            vmem((depth, features), bf16),
+            vmem((6, rows, features), bf16),
+            vmem((2, n_d, n_t, half, depth), bf16),
+            vmem((2, n_d, rows, features), bf16),
+            vmem((2, n_d - 1, rows, features), bf16),
+            vmem((n_d, n_t, half, features), bf16),
+            vmem((n_d, n_t, half, depth), jnp.float32),
+            vmem((n_d, half, depth), bf16),
+            vmem((n_d, half, depth), bf16),
+            vmem((n_d, half, depth), bf16),
+            vmem((per, n_t, half, depth), bf16),
+            vmem((4, rows, features), bf16),
+            vmem((depth, features), bf16),
+            dma((6,)), dma((6,)),
+            dma((2, n_t * per)), dma((2, n_d)),
+            dma((2, n_d)), dma((2, n_d)),
+            dma((2, n_d - 1)), dma((2, n_d - 1)),
+            dma((n_d - 1,)), dma((n_d - 1,)),
+            dma(()), dma(()),
+            dma((n_d,)), dma((per, n_t)),
+            dma(()), dma((7,)),
+        ],
+        compiler_params=pltpu.CompilerParams(
+            collective_id=0, has_side_effects=True, vmem_limit_bytes=62 * 2**20
+        ),
+    )(lengths, sent_out, sent_back, sent_grad, weight)
+
+
+def local(sizes, sent_out, sent_back, sent_grad, lengths, weight):
+    n_s, n_d, n_t = sizes
+    rows, features = sent_out.shape[2:]
+    depth = weight.shape[1]
+    fits = n_s > 2 and n_t == 2 and rows % 32 == 0 and features % depth == 0 and depth % 256 == 0
+    if fits and features % 512 == 0:
+        return tuple(together((n_d, n_t), sent_out, sent_back, sent_grad, lengths, weight))
+    return spread(sent_out, sent_back, sent_grad, lengths, weight)
+
+
 def solution(mesh):
     return jax.shard_map(
-        local,
+        functools.partial(local, tuple(mesh.shape[a] for a in ("section", "dp", "tensor"))),
         mesh=mesh,
         in_specs=(
             P("section", None, "dp", "tensor"),

time: 289 us -> 200 us (0.69)
  Pallas kernels: 0 us -> 190 us
  waiting for transfers between devices: 117 us -> 0 us
  blocking collectives: 91.6 us -> 0 us
  matrix products: 21.1 us -> 0 us
  between operations: 14.9 us -> 1.31 us
  local copies, waits for them, and re-layouts: 21.4 us -> 8.22 us
  starting transfers between devices: 12.8 us -> 0 us
  other arithmetic: 10.2 us -> 0 us
    pallas_call x0 -> x1, Pallas kernels: none -> 190 us  [together(): pl.pallas_call(step_kernel, out_shape=[jax.ShapeDtypeStruct(a.shape, bf16...]
    all_to_all x3 -> x0, blocking collectives: 91.6 us -> none  [the longest x2 52.7 us: shares(): return lax.all_to_all(full, 'dp', split_axis=1, concat_axis=0, tiled=True)]
    ppermute x6 -> x0, waiting for transfers between devices: 85.4 us -> none  [shifted(): return lax.ppermute(block, axis, route)]
    all_gather x3 -> x0, waiting for transfers between devices: 31.4 us -> none  [the longest x1 19.6 us: local(): hidden_all = lax.all_gather(hidden, 'dp', axis=0, tiled=True)]
    dot_general x4 -> x0, matrix products: 21.1 us -> none  [the longest x2 9.48 us: project(): partial = jnp.dot(share, own_weight, preferred_element_type=jnp.float32)]
    ppermute x6 -> x0, starting transfers between devices: 12.5 us -> none  [shifted(): return lax.ppermute(block, axis, route)]
    all_to_all x3 -> x0, local copies, waits for them, and re-layouts: 4.69 us -> none  [the longest x2 3.39 us: shares(): return lax.all_to_all(full, 'dp', split_axis=1, concat_axis=0, tiled=True)]
    squeeze x3 -> x0, local copies, waits for them, and re-layouts: 4.41 us -> none  [the longest x1 2.43 us: local(): back_upper = shifted(sent_back[0, 0], 'section', -1)]
  transfers between devices with their start and end apart: 12 -> 0, of which waited for: 7 -> 0; matrix products, arithmetic and copies ran while one was open for 12% -> 0% of each run, Pallas kernels for 0% -> 0%
where the time goes in v2:
time: 200 us
  Pallas kernels  190 us (95%)
  local copies, waits for them, and re-layouts  8.22 us (4%)
    pallas_call x1, Pallas kernels, together(): pl.pallas_call(step_kernel, out_shape=[jax.ShapeDtypeStruct(a.shape, bf16...  190 us
    unnamed x10, local copies, waits for them, and re-layouts  8.22 us

profile of v2, /device:TPU:0, one launch (start us, length us, event | category | flops | bytes accessed | tf_op | source)
XLA Modules:
  0.0 199.6 jit_solution(15242254431222238789)
XLA Ops:
  1.3 190.1 %shard_map.84 = (bf16[1,2,192,2048]{3,2,1,0:T(8,128)(2,1)}, bf16[1,2,192,2048]{3,2,1,0:T(8,128)(2,1)}, bf16[1,2,192,2048]{3,2,1,0:T(8,128)(2,1)}, bf16[1,1024,2048]{2,1,0:T(8,128)(2,1)}) custom-call(s32[1,1]{1,0:T(1,128)S(6)} %copy.13.lengths, bf16[1,2,192,2048]{3,2,1,0:T(8,128)(2,1)} %sent_out.1, bf16[1,2,192,2048]{3,2,1,0:T(8,128)(2,1)} %sent_back.1, ...), custom_call_target="tpu_custom_call" | custom-call | tf_op jit(solution)/shard_map/pallas_call | solution.py:366
  191.4 0.0 copy-start.2
  191.4 0.0 copy-start.1
  191.4 2.9 %copy.14 = bf16[1,2,192,2048]{3,2,1,0:T(8,128)(2,1)} copy(bf16[1,2,192,2048]{3,2,1,0:T(8,128)(2,1)} %get-tuple-element.8) | data formatting | bytes 3145728
  194.3 0.0 copy-done.2
  194.3 0.0 copy-start
  194.3 1.1 copy.15
  195.4 0.0 copy-done.1
  195.4 1.1 copy.16
  196.5 1.0 copy-done
  197.6 2.0 %copy.17 = bf16[1,1024,2048]{2,1,0:T(8,128)(2,1)} copy(bf16[1,1024,2048]{2,1,0:T(8,128)(2,1)S(1)} %copy-done) | data formatting | bytes 8388608
Async XLA Ops:
  191.4 2.9 %copy-start.2 = (bf16[1,2,192,2048]{3,2,1,0:T(8,128)(2,1)S(1)}, bf16[1,2,192,2048]{3,2,1,0:T(8,128)(2,1)}, u32[]{:S(2)}) copy-start(bf16[1,2,192,2048]{3,2,1,0:T(8,128)(2,1)} %get-tuple-element.9) | copy-start | bytes 4718596
  191.4 4.0 %copy-start.1 = (bf16[1,2,192,2048]{3,2,1,0:T(8,128)(2,1)S(1)}, bf16[1,2,192,2048]{3,2,1,0:T(8,128)(2,1)}, u32[]{:S(2)}) copy-start(bf16[1,2,192,2048]{3,2,1,0:T(8,128)(2,1)} %get-tuple-element.10) | copy-start | bytes 4718596
  194.3 3.3 %copy-start = (bf16[1,1024,2048]{2,1,0:T(8,128)(2,1)S(1)}, bf16[1,1024,2048]{2,1,0:T(8,128)(2,1)}, u32[]{:S(2)}) copy-start(bf16[1,1024,2048]{2,1,0:T(8,128)(2,1)} %get-tuple-element.11) | copy-start | bytes 12582916

commit v3 on v2

--- a/solution.py
+++ b/solution.py
@@ -125,9 +125,6 @@
     along_z(BACK_LOWER).start()
     w_copy = pltpu.make_async_copy(weight.at[0], w, w_sem)
     w_copy.start()
-    along_z(GRAD_UPPER).start()
-    along_z(BACK_UPPER).start()
-    along_z(GRAD_LOWER).start()
 
     def deal(i, x, finish):
         for h in range(n_t):
@@ -208,6 +205,7 @@
     ]
 
     along_z(BACK_LOWER).wait_recv()
+    along_z(GRAD_UPPER).start()
     along_z(OUT_UPPER).start()
     deal(BACK_LOWER, 0, False)
     outs[0].start()
@@ -216,13 +214,13 @@
     multiply(0, True)
 
     along_z(OUT_UPPER).wait_recv()
-    along_z(OUT_LOWER).start()
     deal(OUT_UPPER, 1, False)
     outs[1].start()
-    gather(1)
-    multiply(1, False)
 
     along_z(GRAD_UPPER).wait_recv()
+    along_z(BACK_UPPER).start()
+    along_z(OUT_LOWER).start()
+    along_z(GRAD_LOWER).start()
     for k in range(1, n_d):
         partial(0, k).wait_recv()
     live = lengths[0, 0]
@@ -241,13 +239,30 @@
 
     tiles(hide)
 
-    def show(k):
-        return remote(
-            hidden.at[me_d], hidden.at[me_d], h_send.at[k - 1], h_recv.at[k - 1], (me_s, replica(k), me_t)
-        )
-
-    for k in range(1, n_d):
-        show(k).start()
+    side = lax.rem(me_d, 2)
+    x_near = me_d + 1 - 2 * side
+    y_near = lax.rem(me_d + 2, n_d)
+    far = lax.rem(x_near + 2, n_d)
+
+    def show(n):
+        r, h, target = (
+            (me_d, 0, x_near), (me_d, 1, y_near), (me_d, 1, x_near),
+            (me_d, 0, y_near), (x_near, 0, y_near), (y_near, 1, x_near),
+        )[n]
+        block = hidden.at[r, h]
+        return remote(block, block, h_send.at[n], h_recv.at[n], (me_s, target, me_t))
+
+    def shown(n):
+        r, h = ((x_near, 0), (y_near, 1), (x_near, 1), (y_near, 0), (far, 0), (far, 1))[n]
+        landed(hidden.at[r, h], h_recv.at[n])
+
+    for n in range(4):
+        show(n).start()
+    gather(1)
+    multiply(1, False)
+    for n in range(2):
+        shown(n)
+        show(n + 4).start()
     for k in range(1, n_d):
         partial(1, k).start()
     outs[2].start()
@@ -262,8 +277,8 @@
     tiles(rebuild)
     outs[3].start()
 
-    for k in range(1, n_d):
-        landed(hidden.at[replica(-k)], h_recv.at[k - 1])
+    for n in range(2, 6):
+        shown(n)
 
     @pl.loop(0, depth // 256)
     def _(c):
@@ -346,8 +361,8 @@
             relay(x, k).wait_send()
         for k in range(1, n_d):
             partial(x, k).wait_send()
-    for k in range(1, n_d):
-        show(k).wait_send()
+    for n in range(6):
+        show(n).wait_send()
     swap.wait_send()
     for k in range(n_d):
         back_to(k, True)
@@ -386,7 +401,7 @@
             dma((2, n_t * per)), dma((2, n_d)),
             dma((2, n_d)), dma((2, n_d)),
             dma((2, n_d - 1)), dma((2, n_d - 1)),
-            dma((n_d - 1,)), dma((n_d - 1,)),
+            dma((6,)), dma((6,)),
             dma(()), dma(()),
             dma((n_d,)), dma((per, n_t)),
             dma(()), dma((7,)),
@@ -401,7 +416,7 @@
     n_s, n_d, n_t = sizes
     rows, features = sent_out.shape[2:]
     depth = weight.shape[1]
-    fits = n_s > 2 and n_t == 2 and rows % 32 == 0 and features % depth == 0 and depth % 256 == 0
+    fits = n_s > 2 and n_d == 4 and n_t == 2 and rows % 32 == 0 and features % depth == 0 and depth % 256 == 0
     if fits and features % 512 == 0:
         return tuple(together((n_d, n_t), sent_out, sent_back, sent_grad, lengths, weight))
     return spread(sent_out, sent_back, sent_grad, lengths, weight)

time: 200 us -> 159 us (0.80)
  Pallas kernels: 190 us -> 149 us
    pallas_call x1, Pallas kernels: 190 us -> 149 us  [together(): pl.pallas_call(step_kernel, out_shape=[jax.ShapeDtypeStruct(a.shape, bf16...]
where the time goes in v3:
time: 159 us
  Pallas kernels  149 us (94%)
  local copies, waits for them, and re-layouts  8.22 us (5%)
    pallas_call x1, Pallas kernels, together(): pl.pallas_call(step_kernel, out_shape=[jax.ShapeDtypeStruct(a.shape, bf16...  149 us
    unnamed x10, local copies, waits for them, and re-layouts  8.22 us

profile of v3, /device:TPU:0, one launch (start us, length us, event | category | flops | bytes accessed | tf_op | source)
XLA Modules:
  0.0 158.7 jit_solution(4010002613148453822)
XLA Ops:
  1.3 149.2 %shard_map.84 = (bf16[1,2,192,2048]{3,2,1,0:T(8,128)(2,1)}, bf16[1,2,192,2048]{3,2,1,0:T(8,128)(2,1)}, bf16[1,2,192,2048]{3,2,1,0:T(8,128)(2,1)}, bf16[1,1024,2048]{2,1,0:T(8,128)(2,1)}) custom-call(s32[1,1]{1,0:T(1,128)S(6)} %copy.13.lengths, bf16[1,2,192,2048]{3,2,1,0:T(8,128)(2,1)} %sent_out.1, bf16[1,2,192,2048]{3,2,1,0:T(8,128)(2,1)} %sent_back.1, ...), custom_call_target="tpu_custom_call" | custom-call | tf_op jit(solution)/shard_map/pallas_call | solution.py:381
  150.5 0.0 copy-start.2
  150.5 0.0 copy-start.1
  150.5 2.9 %copy.14 = bf16[1,2,192,2048]{3,2,1,0:T(8,128)(2,1)} copy(bf16[1,2,192,2048]{3,2,1,0:T(8,128)(2,1)} %get-tuple-element.8) | data formatting | bytes 3145728
  153.4 0.0 copy-done.2
  153.4 0.0 copy-start
  153.4 1.1 copy.15
  154.5 0.0 copy-done.1
  154.5 1.1 copy.16
  155.7 1.0 copy-done
  156.7 2.0 %copy.17 = bf16[1,1024,2048]{2,1,0:T(8,128)(2,1)} copy(bf16[1,1024,2048]{2,1,0:T(8,128)(2,1)S(1)} %copy-done) | data formatting | bytes 8388608
Async XLA Ops:
  150.5 2.9 %copy-start.2 = (bf16[1,2,192,2048]{3,2,1,0:T(8,128)(2,1)S(1)}, bf16[1,2,192,2048]{3,2,1,0:T(8,128)(2,1)}, u32[]{:S(2)}) copy-start(bf16[1,2,192,2048]{3,2,1,0:T(8,128)(2,1)} %get-tuple-element.9) | copy-start | bytes 4718596
  150.5 4.0 %copy-start.1 = (bf16[1,2,192,2048]{3,2,1,0:T(8,128)(2,1)S(1)}, bf16[1,2,192,2048]{3,2,1,0:T(8,128)(2,1)}, u32[]{:S(2)}) copy-start(bf16[1,2,192,2048]{3,2,1,0:T(8,128)(2,1)} %get-tuple-element.10) | copy-start | bytes 4718596
  153.4 3.3 %copy-start = (bf16[1,1024,2048]{2,1,0:T(8,128)(2,1)S(1)}, bf16[1,1024,2048]{2,1,0:T(8,128)(2,1)}, u32[]{:S(2)}) copy-start(bf16[1,1024,2048]{2,1,0:T(8,128)(2,1)} %get-tuple-element.11) | copy-start | bytes 12582916

commit v4 on v3

--- a/solution.py
+++ b/solution.py
@@ -80,7 +80,7 @@
     lengths, sent_out, sent_back, sent_grad, weight,
     emitted, rebuilt, grads_out, weight_grad,
     w, got, share, part, summed, hidden, terms, tx, trx, ts, tr, stage, wg,
-    z_send, z_recv, d_send, d_recv, r_send, r_recv, p_send, p_recv,
+    z_send, z_recv, b_send, b_recv, d_send, d_recv, r_send, r_recv, p_send, p_recv,
     h_send, h_recv, t_send, t_recv, f_send, f_recv, w_sem, o_sem,
 ):
     f32, bf16 = jnp.float32, jnp.bfloat16
@@ -95,6 +95,11 @@
     def replica(k):
         return lax.rem(me_d + k + n_d, n_d)
 
+    side = lax.rem(me_d, 2)
+    x_near = me_d + 1 - 2 * side
+    y_near = lax.rem(me_d + 2, n_d)
+    far = lax.rem(x_near + 2, n_d)
+
     barrier = pltpu.get_barrier_semaphore()
     for k in range(n_d):
         for c in range(n_t):
@@ -122,7 +127,15 @@
         }[i]
         return remote(src.at[0, piece], got.at[i], z_send.at[i], z_recv.at[i], (z, me_d, me_t))
 
-    along_z(BACK_LOWER).start()
+    def back_lower(n):
+        h, j = n // per, n % per
+        piece = (pl.ds(h * half, half), pl.ds(j * depth, depth))
+        return remote(
+            sent_back.at[0, 1, *piece], got.at[BACK_LOWER, *piece], b_send.at[n], b_recv.at[n], (prv, me_d, me_t)
+        )
+
+    for n in range(n_t * per):
+        back_lower(n).start()
     w_copy = pltpu.make_async_copy(weight.at[0], w, w_sem)
     w_copy.start()
 
@@ -130,6 +143,8 @@
         for h in range(n_t):
             for j in range(per):
                 n = h * per + j
+                if i == BACK_LOWER and not finish:
+                    back_lower(n).wait_recv()
                 target = me_t * per + j
                 src = got.at[i, pl.ds(h * half, half), pl.ds(j * depth, depth)]
                 dst = share.at[x, me_d, h]
@@ -154,11 +169,28 @@
             share.at[x, r, me_t], share.at[x, r, me_t], r_send.at[x, r], r_recv.at[x, r], (me_s, me_d, other)
         )
 
-    def partial(x, k):
-        r = replica(k)
+    wide = local_features // 2
+
+    def partial(x, n):
+        r, side_of, target = (
+            (far, 0, x_near), (far, 1, y_near), (x_near, 0, x_near),
+            (y_near, 1, y_near), (y_near, 0, y_near), (x_near, 1, x_near),
+        )[n]
         return remote(
-            part.at[x, r], summed.at[x, k - 1], p_send.at[x, k - 1], p_recv.at[x, k - 1], (me_s, r, me_t)
+            part.at[x, r, :, pl.ds(side_of * wide, wide)], summed.at[x, n],
+            p_send.at[x, n], p_recv.at[x, n], (me_s, target, me_t),
         )
+
+    def combine(x):
+        for n in range(2):
+            r = (y_near, x_near)[n]
+            partial(x, n).wait_recv()
+            for c in range(wide // 256):
+                near = pl.ds(c * 256, 256)
+                cols = pl.ds(n * wide + c * 256, 256)
+                both = part[x, r, :, cols].astype(f32) + summed[x, n, :, near].astype(f32)
+                part[x, r, :, cols] = both.astype(bf16)
+            partial(x, n + 4).start()
 
     def gather(x):
         for k in range(n_d):
@@ -168,8 +200,7 @@
             landed(share.at[x, replica(k), other], r_recv.at[x, replica(k)])
 
     def multiply(x, send):
-        for k in list(range(1, n_d)) + [0]:
-            r = replica(k)
+        for k, r in enumerate((far, x_near, y_near, me_d)):
 
             @pl.loop(0, local_features // 512)
             def _(c):
@@ -177,19 +208,21 @@
                 left = share[x, r].reshape(rows, depth)
                 part[x, r, :, cols] = jnp.dot(left, w[:, cols], preferred_element_type=f32).astype(bf16)
 
-            if send and k:
-                partial(x, k).start()
-
-    def total(x, cols):
+            if send:
+                for n in ((0, 1), (2,), (3,), ())[k]:
+                    partial(x, n).start()
+
+    def total(x, c):
+        cols = pl.ds(pl.multiple_of(c * 256, 256), 256)
+        n = lax.div(c, wide // 256)
+        near = pl.ds(pl.multiple_of(lax.rem(c, wide // 256) * 256, 256), 256)
         pre = part[x, me_d, :, cols].astype(f32)
-        for k in range(n_d - 1):
-            pre = pre + summed[x, k, :, cols].astype(f32)
-        return pre
+        return pre + summed[x, 2 + n, :, near].astype(f32) + summed[x, 4 + n, :, near].astype(f32)
 
     def tiles(body):
         @pl.loop(0, local_features // 256)
         def _(c):
-            body(pl.ds(pl.multiple_of(c * 256, 256), 256))
+            body(c, pl.ds(pl.multiple_of(c * 256, 256), 256))
 
     def out(i, src, dst):
         return pltpu.make_async_copy(src, dst, o_sem.at[i])
@@ -204,14 +237,14 @@
         out(6, wg, weight_grad.at[0]),
     ]
 
-    along_z(BACK_LOWER).wait_recv()
+    deal(BACK_LOWER, 0, False)
     along_z(GRAD_UPPER).start()
     along_z(OUT_UPPER).start()
-    deal(BACK_LOWER, 0, False)
     outs[0].start()
     gather(0)
     w_copy.wait()
     multiply(0, True)
+    combine(0)
 
     along_z(OUT_UPPER).wait_recv()
     deal(OUT_UPPER, 1, False)
@@ -221,16 +254,16 @@
     along_z(BACK_UPPER).start()
     along_z(OUT_LOWER).start()
     along_z(GRAD_LOWER).start()
-    for k in range(1, n_d):
-        partial(0, k).wait_recv()
+    for n in range(2, 6):
+        partial(0, n).wait_recv()
     live = lengths[0, 0]
 
     def keep(block):
         place = lax.broadcasted_iota(jnp.int32, block.shape, 0)
         return jnp.where(place < live, block.astype(f32), 0.0)
 
-    def hide(cols):
-        pre = total(0, cols)
+    def hide(c, cols):
+        pre = total(0, c)
         dupper = keep(got[GRAD_UPPER, :, cols])
         stage[0, :, cols] = dupper.astype(bf16)
         sigma = jax.nn.sigmoid(pre)
@@ -238,11 +271,6 @@
         hidden[me_d, :, :, cols] = gated.reshape(n_t, half, 256)
 
     tiles(hide)
-
-    side = lax.rem(me_d, 2)
-    x_near = me_d + 1 - 2 * side
-    y_near = lax.rem(me_d + 2, n_d)
-    far = lax.rem(x_near + 2, n_d)
 
     def show(n):
         r, h, target = (
@@ -263,14 +291,14 @@
     for n in range(2):
         shown(n)
         show(n + 4).start()
-    for k in range(1, n_d):
-        partial(1, k).start()
+    for n in range(4):
+        partial(1, n).start()
     outs[2].start()
 
     along_z(BACK_UPPER).wait_recv()
 
-    def rebuild(cols):
-        pre = total(0, cols)
+    def rebuild(c, cols):
+        pre = total(0, c)
         upper = got[BACK_UPPER, :, cols].astype(f32)
         stage[1, :, cols] = (upper - pre * jax.nn.sigmoid(pre)).astype(bf16)
 
@@ -291,6 +319,7 @@
         tx[r] = terms[r, other].astype(bf16)
     swap = remote(tx, trx, t_send, t_recv, (me_s, me_d, other))
     swap.start()
+    combine(1)
 
     def weigh(lo, hi):
         @pl.loop(lo, hi)
@@ -331,11 +360,11 @@
     outs[6].start()
 
     along_z(OUT_LOWER).wait_recv()
-    for k in range(1, n_d):
-        partial(1, k).wait_recv()
-
-    def emit(cols):
-        pre = total(1, cols)
+    for n in range(2, 6):
+        partial(1, n).wait_recv()
+
+    def emit(c, cols):
+        pre = total(1, c)
         lower = got[OUT_LOWER, :, cols].astype(f32)
         stage[2, :, cols] = (lower + pre * jax.nn.sigmoid(pre)).astype(bf16)
 
@@ -353,14 +382,16 @@
         stage[3, :, span] = (keep(got[GRAD_LOWER, :, span]) + through).astype(bf16)
     outs[5].start()
 
-    for i in range(6):
+    for n in range(n_t * per):
+        back_lower(n).wait_send()
+    for i in range(1, 6):
         along_z(i).wait_send()
     for x, i in ((0, BACK_LOWER), (1, OUT_UPPER)):
         deal(i, x, True)
         for k in range(n_d):
             relay(x, k).wait_send()
-        for k in range(1, n_d):
-            partial(x, k).wait_send()
+        for n in range(6):
+            partial(x, n).wait_send()
     for n in range(6):
         show(n).wait_send()
     swap.wait_send()
@@ -388,7 +419,7 @@
             vmem((6, rows, features), bf16),
             vmem((2, n_d, n_t, half, depth), bf16),
             vmem((2, n_d, rows, features), bf16),
-            vmem((2, n_d - 1, rows, features), bf16),
+            vmem((2, 6, rows, features // 2), bf16),
             vmem((n_d, n_t, half, features), bf16),
             vmem((n_d, n_t, half, depth), jnp.float32),
             vmem((n_d, half, depth), bf16),
@@ -398,9 +429,10 @@
             vmem((4, rows, features), bf16),
             vmem((depth, features), bf16),
             dma((6,)), dma((6,)),
+            dma((n_t * per,)), dma((n_t * per,)),
             dma((2, n_t * per)), dma((2, n_d)),
             dma((2, n_d)), dma((2, n_d)),
-            dma((2, n_d - 1)), dma((2, n_d - 1)),
+            dma((2, 6)), dma((2, 6)),
             dma((6,)), dma((6,)),
             dma(()), dma(()),
             dma((n_d,)), dma((per, n_t)),

time: 159 us -> 140 us (0.88)
  Pallas kernels: 149 us -> 130 us
    pallas_call x1, Pallas kernels: 149 us -> 130 us  [together(): pl.pallas_call(step_kernel, out_shape=[jax.ShapeDtypeStruct(a.shape, bf16...]
where the time goes in v4:
time: 140 us
  Pallas kernels  130 us (93%)
  local copies, waits for them, and re-layouts  8.22 us (6%)
    pallas_call x1, Pallas kernels, together(): pl.pallas_call(step_kernel, out_shape=[jax.ShapeDtypeStruct(a.shape, bf16...  130 us
    unnamed x10, local copies, waits for them, and re-layouts  8.22 us

profile of v4, /device:TPU:0, one launch (start us, length us, event | category | flops | bytes accessed | tf_op | source)
XLA Modules:
  0.0 140.0 jit_solution(2748755503556727384)
XLA Ops:
  1.3 130.5 %shard_map.84 = (bf16[1,2,192,2048]{3,2,1,0:T(8,128)(2,1)}, bf16[1,2,192,2048]{3,2,1,0:T(8,128)(2,1)}, bf16[1,2,192,2048]{3,2,1,0:T(8,128)(2,1)}, bf16[1,1024,2048]{2,1,0:T(8,128)(2,1)}) custom-call(s32[1,1]{1,0:T(1,128)S(6)} %copy.13.lengths, bf16[1,2,192,2048]{3,2,1,0:T(8,128)(2,1)} %sent_out.1, bf16[1,2,192,2048]{3,2,1,0:T(8,128)(2,1)} %sent_back.1, ...), custom_call_target="tpu_custom_call" | custom-call | tf_op jit(solution)/shard_map/pallas_call | solution.py:412
  131.8 0.0 copy-start.2
  131.8 0.0 copy-start.1
  131.8 2.9 %copy.14 = bf16[1,2,192,2048]{3,2,1,0:T(8,128)(2,1)} copy(bf16[1,2,192,2048]{3,2,1,0:T(8,128)(2,1)} %get-tuple-element.8) | data formatting | bytes 3145728
  134.7 0.0 copy-done.2
  134.7 0.0 copy-start
  134.7 1.1 copy.15
  135.8 0.0 copy-done.1
  135.8 1.1 copy.16
  137.0 1.0 copy-done
  138.0 2.0 %copy.17 = bf16[1,1024,2048]{2,1,0:T(8,128)(2,1)} copy(bf16[1,1024,2048]{2,1,0:T(8,128)(2,1)S(1)} %copy-done) | data formatting | bytes 8388608
Async XLA Ops:
  131.8 2.9 %copy-start.2 = (bf16[1,2,192,2048]{3,2,1,0:T(8,128)(2,1)S(1)}, bf16[1,2,192,2048]{3,2,1,0:T(8,128)(2,1)}, u32[]{:S(2)}) copy-start(bf16[1,2,192,2048]{3,2,1,0:T(8,128)(2,1)} %get-tuple-element.9) | copy-start | bytes 4718596
  131.8 4.0 %copy-start.1 = (bf16[1,2,192,2048]{3,2,1,0:T(8,128)(2,1)S(1)}, bf16[1,2,192,2048]{3,2,1,0:T(8,128)(2,1)}, u32[]{:S(2)}) copy-start(bf16[1,2,192,2048]{3,2,1,0:T(8,128)(2,1)} %get-tuple-element.10) | copy-start | bytes 4718596
  134.7 3.3 %copy-start = (bf16[1,1024,2048]{2,1,0:T(8,128)(2,1)S(1)}, bf16[1,1024,2048]{2,1,0:T(8,128)(2,1)}, u32[]{:S(2)}) copy-start(bf16[1,1024,2048]{2,1,0:T(8,128)(2,1)} %get-tuple-element.11) | copy-start | bytes 12582916

commit v5 on v4

--- a/solution.py
+++ b/solution.py
@@ -199,7 +199,7 @@
         for k in range(n_d):
             landed(share.at[x, replica(k), other], r_recv.at[x, replica(k)])
 
-    def multiply(x, send):
+    def multiply(x):
         for k, r in enumerate((far, x_near, y_near, me_d)):
 
             @pl.loop(0, local_features // 512)
@@ -208,9 +208,8 @@
                 left = share[x, r].reshape(rows, depth)
                 part[x, r, :, cols] = jnp.dot(left, w[:, cols], preferred_element_type=f32).astype(bf16)
 
-            if send:
-                for n in ((0, 1), (2,), (3,), ())[k]:
-                    partial(x, n).start()
+            for n in ((0, 1), (2,), (3,), ())[k]:
+                partial(x, n).start()
 
     def total(x, c):
         cols = pl.ds(pl.multiple_of(c * 256, 256), 256)
@@ -239,21 +238,13 @@
 
     deal(BACK_LOWER, 0, False)
     along_z(GRAD_UPPER).start()
-    along_z(OUT_UPPER).start()
     outs[0].start()
     gather(0)
     w_copy.wait()
-    multiply(0, True)
+    multiply(0)
+    along_z(GRAD_UPPER).wait_recv()
+    along_z(OUT_UPPER).start()
     combine(0)
-
-    along_z(OUT_UPPER).wait_recv()
-    deal(OUT_UPPER, 1, False)
-    outs[1].start()
-
-    along_z(GRAD_UPPER).wait_recv()
-    along_z(BACK_UPPER).start()
-    along_z(OUT_LOWER).start()
-    along_z(GRAD_LOWER).start()
     for n in range(2, 6):
         partial(0, n).wait_recv()
     live = lengths[0, 0]
@@ -286,13 +277,17 @@
 
     for n in range(4):
         show(n).start()
-    gather(1)
-    multiply(1, False)
+    along_z(OUT_UPPER).wait_recv()
+    along_z(BACK_UPPER).start()
+    along_z(OUT_LOWER).start()
+    along_z(GRAD_LOWER).start()
+    deal(OUT_UPPER, 1, False)
+    outs[1].start()
     for n in range(2):
         shown(n)
         show(n + 4).start()
-    for n in range(4):
-        partial(1, n).start()
+    gather(1)
+    multiply(1)
     outs[2].start()
 
     along_z(BACK_UPPER).wait_recv()

time: 140 us -> 138 us (0.986)
    pallas_call x1, Pallas kernels: 130 us -> 129 us  [together(): pl.pallas_call(step_kernel, out_shape=[jax.ShapeDtypeStruct(a.shape, bf16...]
where the time goes in v5:
time: 138 us
  Pallas kernels  129 us (93%)
  local copies, waits for them, and re-layouts  8.22 us (6%)
    pallas_call x1, Pallas kernels, together(): pl.pallas_call(step_kernel, out_shape=[jax.ShapeDtypeStruct(a.shape, bf16...  129 us
    unnamed x10, local copies, waits for them, and re-layouts  8.22 us

profile of v5, /device:TPU:0, one launch (start us, length us, event | category | flops | bytes accessed | tf_op | source)
XLA Modules:
  0.0 138.1 jit_solution(66785788519601483)
XLA Ops:
  1.3 128.5 %shard_map.84 = (bf16[1,2,192,2048]{3,2,1,0:T(8,128)(2,1)}, bf16[1,2,192,2048]{3,2,1,0:T(8,128)(2,1)}, bf16[1,2,192,2048]{3,2,1,0:T(8,128)(2,1)}, bf16[1,1024,2048]{2,1,0:T(8,128)(2,1)}) custom-call(s32[1,1]{1,0:T(1,128)S(6)} %copy.13.lengths, bf16[1,2,192,2048]{3,2,1,0:T(8,128)(2,1)} %sent_out.1, bf16[1,2,192,2048]{3,2,1,0:T(8,128)(2,1)} %sent_back.1, ...), custom_call_target="tpu_custom_call" | custom-call | tf_op jit(solution)/shard_map/pallas_call | solution.py:407
  129.8 0.0 copy-start.2
  129.8 0.0 copy-start.1
  129.8 2.9 %copy.14 = bf16[1,2,192,2048]{3,2,1,0:T(8,128)(2,1)} copy(bf16[1,2,192,2048]{3,2,1,0:T(8,128)(2,1)} %get-tuple-element.8) | data formatting | bytes 3145728
  132.7 0.0 copy-done.2
  132.7 0.0 copy-start
  132.7 1.1 copy.15
  133.9 0.0 copy-done.1
  133.9 1.1 copy.16
  135.0 1.0 copy-done
  136.1 2.0 %copy.17 = bf16[1,1024,2048]{2,1,0:T(8,128)(2,1)} copy(bf16[1,1024,2048]{2,1,0:T(8,128)(2,1)S(1)} %copy-done) | data formatting | bytes 8388608
Async XLA Ops:
  129.8 2.9 %copy-start.2 = (bf16[1,2,192,2048]{3,2,1,0:T(8,128)(2,1)S(1)}, bf16[1,2,192,2048]{3,2,1,0:T(8,128)(2,1)}, u32[]{:S(2)}) copy-start(bf16[1,2,192,2048]{3,2,1,0:T(8,128)(2,1)} %get-tuple-element.9) | copy-start | bytes 4718596
  129.8 4.0 %copy-start.1 = (bf16[1,2,192,2048]{3,2,1,0:T(8,128)(2,1)S(1)}, bf16[1,2,192,2048]{3,2,1,0:T(8,128)(2,1)}, u32[]{:S(2)}) copy-start(bf16[1,2,192,2048]{3,2,1,0:T(8,128)(2,1)} %get-tuple-element.10) | copy-start | bytes 4718596
  132.7 3.3 %copy-start = (bf16[1,1024,2048]{2,1,0:T(8,128)(2,1)S(1)}, bf16[1,1024,2048]{2,1,0:T(8,128)(2,1)}, u32[]{:S(2)}) copy-start(bf16[1,1024,2048]{2,1,0:T(8,128)(2,1)} %get-tuple-element.11) | copy-start | bytes 12582916

commit v6 on v5

--- a/solution.py
+++ b/solution.py
@@ -434,7 +434,7 @@
             dma(()), dma((7,)),
         ],
         compiler_params=pltpu.CompilerParams(
-            collective_id=0, has_side_effects=True, vmem_limit_bytes=62 * 2**20
+            collective_id=0, has_side_effects=True, vmem_limit_bytes=50 * 2**20
         ),
     )(lengths, sent_out, sent_back, sent_grad, weight)
 

time: 138 us -> 137 us (level)
  local copies, waits for them, and re-layouts: 8.22 us -> 6.6 us
    unnamed x10 -> x8, local copies, waits for them, and re-layouts: 8.22 us -> 6.6 us
where the time goes in v6:
time: 137 us; the launch traced here: 136 us
  Pallas kernels  129 us (94%)
  local copies, waits for them, and re-layouts  6.6 us (5%)
    pallas_call x1, Pallas kernels, together(): pl.pallas_call(step_kernel, out_shape=[jax.ShapeDtypeStruct(a.shape, bf16...  129 us
    unnamed x8, local copies, waits for them, and re-layouts  6.6 us

profile of v6, /device:TPU:0, one launch (start us, length us, event | category | flops | bytes accessed | tf_op | source)
XLA Modules:
  0.0 136.4 jit_solution(17789773795751877727)
XLA Ops:
  1.3 128.5 %shard_map.84 = (bf16[1,2,192,2048]{3,2,1,0:T(8,128)(2,1)S(1)}, bf16[1,2,192,2048]{3,2,1,0:T(8,128)(2,1)S(1)}, bf16[1,2,192,2048]{3,2,1,0:T(8,128)(2,1)}, bf16[1,1024,2048]{2,1,0:T(8,128)(2,1)}) custom-call(s32[1,1]{1,0:T(1,128)S(6)} %copy.13.lengths, bf16[1,2,192,2048]{3,2,1,0:T(8,128)(2,1)} %sent_out.1, bf16[1,2,192,2048]{3,2,1,0:T(8,128)(2,1)} %sent_back.1, ...), custom_call_target="tpu_custom_call" | custom-call | tf_op jit(solution)/shard_map/pallas_call | solution.py:407
  129.8 0.0 copy-start.1
  129.8 1.1 copy.14
  131.0 0.0 copy-start
  131.0 1.1 copy.15
  132.1 0.0 copy-done.1
  132.1 1.1 copy.16
  133.3 1.2 copy-done
  134.4 2.0 %copy.17 = bf16[1,1024,2048]{2,1,0:T(8,128)(2,1)} copy(bf16[1,1024,2048]{2,1,0:T(8,128)(2,1)S(1)} %copy-done) | data formatting | bytes 8388608
Async XLA Ops:
  129.8 2.3 %copy-start.1 = (bf16[1,2,192,2048]{3,2,1,0:T(8,128)(2,1)S(1)}, bf16[1,2,192,2048]{3,2,1,0:T(8,128)(2,1)}, u32[]{:S(2)}) copy-start(bf16[1,2,192,2048]{3,2,1,0:T(8,128)(2,1)} %get-tuple-element.10) | copy-start | bytes 4718596
  131.0 3.4 %copy-start = (bf16[1,1024,2048]{2,1,0:T(8,128)(2,1)S(1)}, bf16[1,1024,2048]{2,1,0:T(8,128)(2,1)}, u32[]{:S(2)}) copy-start(bf16[1,1024,2048]{2,1,0:T(8,128)(2,1)} %get-tuple-element.11) | copy-start | bytes 12582916
